TPU v7x, 32 devices: a whole 2x2x4 slice. The times are simulated.
32 devices in a mesh: span: 8 (over z, x), tensor: 4 (over y, core).
Axes of the slice: x: 2, y: 2, z: 4, core: 2. Of those that a mesh axis runs over, the one named last changes fastest.
Arguments:
- latents: bfloat16 [1024, 5120], P(('span', 'tensor')), may hold values from -6 to 6
- modulation: float32 [4, 3, 5120], replicated, may hold values from -3 to 3
- w_query: bfloat16 [5120, 4096], P(None, 'tensor'), may hold values from -0.078125 to 0.078125
- w_key: bfloat16 [5120, 4096], P(None, 'tensor'), may hold values from -0.078125 to 0.078125
- w_value: bfloat16 [5120, 4096], P(None, 'tensor'), may hold values from -0.078125 to 0.078125
- w_out: bfloat16 [4096, 5120], P('tensor'), may hold values from -0.5 to 0.5
- cache_k: bfloat16 [2048, 4096], P('span', 'tensor'), may hold values from -800 to 800
- cache_v: bfloat16 [2048, 4096], P('span', 'tensor'), may hold values from -6 to 6
- level_index: int32 [8], P('span'), may hold values from 0 to 3
- rotation: int32 [8], replicated, may hold values from 0 to 7, each once
- cached_tokens: int32 [1], replicated, may hold values from 128 to 2048
Outputs:
- branch: bfloat16 [1024, 5120], P(('span', 'tensor'))
All inputs are finite; a program needn't handle non-finite values.
Results may differ from a plain program's by a relative error of at most 0.019.
Values may be sent and summed in bfloat16 or wider, within the bound.
No kernel may reach another device: no remote copies, remote signals or barrier semaphores. Data moves between devices by JAX's collectives and lax.ppermute only.
A program may use at most 128 MiB of HBM per device.

v0:
```python
import jax
import jax.numpy as jnp
from jax import lax
from jax.sharding import PartitionSpec as P

HD = 128


EPSILON = 1e-06


def block_update(running, q_heads, key_block, value_block, key_valid):
    run_max, run_sum, run_acc = running
    head_count = q_heads.shape[1]
    head_size = q_heads.shape[2]
    key_heads = key_block.reshape(key_block.shape[0], head_count, head_size)
    value_heads = value_block.reshape(value_block.shape[0], head_count, head_size)
    scores = jnp.einsum(
        "qhd,khd->hqk", q_heads, key_heads, preferred_element_type=jnp.float32
    ) * head_size ** (-0.5)
    scores = jnp.where(key_valid[None, None, :], scores, -1e30)
    new_max = jnp.maximum(run_max, jnp.max(scores, axis=-1))
    weights = jnp.where(key_valid[None, None, :], jnp.exp(scores - new_max[..., None]), 0.0)
    rescale = jnp.exp(run_max - new_max)
    run_sum = run_sum * rescale + jnp.sum(weights, axis=-1)
    run_acc = run_acc * rescale[..., None] + jnp.einsum(
        "hqk,khd->hqd",
        weights.astype(jnp.bfloat16),
        value_heads,
        preferred_element_type=jnp.float32,
    )
    return (new_max, run_sum, run_acc)


def attend(running, q_heads, key_rows, value_rows, key_valid):
    running = block_update(running, q_heads, key_rows, value_rows, key_valid)
    return running


def body(
    latents,
    modulation,
    w_query,
    w_key,
    w_value,
    w_out,
    cache_k,
    cache_v,
    level_index,
    rotation,
    cached_tokens,
):
    groups = lax.axis_size("span")
    own_index = lax.axis_index("span")
    chooser = (jnp.arange(modulation.shape[0], dtype=jnp.int32) == level_index[0]).astype(
        jnp.float32
    )
    mod_rows = jnp.sum(chooser[:, None, None] * modulation, axis=0)
    shift_row, scale_row, gate_row = (mod_rows[0], mod_rows[1], mod_rows[2])
    row_data = latents.astype(jnp.float32)
    row_mean = jnp.mean(row_data, axis=-1, keepdims=True)
    centred = row_data - row_mean
    row_var = jnp.mean(centred * centred, axis=-1, keepdims=True)
    normed = centred * lax.rsqrt(row_var + EPSILON)
    modulated = (normed * (1.0 + scale_row) + shift_row).astype(jnp.bfloat16)
    shard_piece = lax.all_gather(modulated, "tensor", axis=0, tiled=True)
    projected = [
        jnp.dot(shard_piece, weight, preferred_element_type=jnp.float32).astype(jnp.bfloat16)
        for weight in (w_query, w_key, w_value)
    ]
    joined = jnp.concatenate(projected, axis=1)
    inner_width = w_query.shape[1]
    own_query = joined[:, :inner_width]
    own_key = joined[:, inner_width : 2 * inner_width]
    own_value = joined[:, 2 * inner_width :]
    head_count = inner_width // HD
    span_rows = own_query.shape[0]
    q_heads = own_query.reshape(span_rows, head_count, HD)
    group_ids = jnp.arange(groups, dtype=jnp.int32)
    order_own = jnp.sum(jnp.where(group_ids == own_index, rotation, 0))
    live_keys = cached_tokens[0]
    initial = (
        jnp.full((head_count, span_rows), -1e30, jnp.float32),
        jnp.zeros((head_count, span_rows), jnp.float32),
        jnp.zeros((head_count, span_rows, HD), jnp.float32),
    )
    all_queries = lax.all_gather(own_query, "span", axis=0, tiled=True)
    cache_rows = cache_k.shape[0]
    local_valid = own_index * cache_rows + jnp.arange(cache_rows, dtype=jnp.int32) < live_keys

    def group_partial(group_queries):
        return attend(initial, group_queries, cache_k, cache_v, local_valid)

    partials = lax.map(group_partial, all_queries.reshape(groups, span_rows, head_count, HD))
    source_max, source_sum, source_acc = lax.all_to_all(
        partials, "span", split_axis=0, concat_axis=0, tiled=True
    )
    best_max = jnp.max(source_max, axis=0)
    rescale = jnp.exp(source_max - best_max)
    running = (
        best_max,
        jnp.sum(source_sum * rescale, axis=0),
        jnp.sum(source_acc * rescale[..., None], axis=0),
    )
    key_rows = lax.all_gather(own_key, "span", axis=0, tiled=True)
    value_rows = lax.all_gather(own_value, "span", axis=0, tiled=True)
    key_index = jnp.arange(key_rows.shape[0], dtype=jnp.int32)
    key_group = key_index // span_rows
    key_order = jnp.sum(
        jnp.where(key_group[:, None] == group_ids[None, :], rotation[None, :], 0), axis=1
    )
    key_valid = key_order <= order_own
    run_max, run_sum, run_acc = attend(running, q_heads, key_rows, value_rows, key_valid)
    attended = (
        (run_acc / run_sum[..., None])
        .transpose(1, 0, 2)
        .reshape(span_rows, inner_width)
        .astype(jnp.bfloat16)
    )
    projection = lax.psum_scatter(
        jnp.dot(attended, w_out, preferred_element_type=jnp.float32).astype(jnp.bfloat16),
        "tensor",
        scatter_dimension=0,
        tiled=True,
    ).astype(jnp.float32)
    return (gate_row[None, :] * projection).astype(jnp.bfloat16)


def solution(mesh):
    placed = (
        P(("span", "tensor"), None),
        P(),
        P(None, "tensor"),
        P(None, "tensor"),
        P(None, "tensor"),
        P("tensor", None),
        P("span", "tensor"),
        P("span", "tensor"),
        P("span"),
        P(),
        P(),
    )
    return jax.shard_map(
        body, mesh=mesh, in_specs=placed, out_specs=P(("span", "tensor"), None), check_vma=False
    )
```

profile of v0, /device:TPU:0, one launch (start us, length us, event | category | flops | bytes accessed | tf_op | source)
XLA Modules:
  0.0 317.0 jit_solution(9142673391689891589)
XLA Ops:
  12.8 21.0 %all-gather.5.cloned.1.call-done = bf16[128,5120]{1,0:T(8,128)(2,1)} async-done(((bf16[32,5120]{1,0:T(8,128)(2,1)}), bf16[128,5120]{1,0:T(8,128)(2,1)}) %all-gather.5.cloned.1.call-update) | async-done | bytes 1310736 | tf_op jit(solution)/shard_map/all_gather | solution.py:66
  33.8 6.7 %convolution_convert_fusion.3 = bf16[128,1024]{1,0:T(8,128)(2,1)} fusion(bf16[128,5120]{1,0:T(8,128)(2,1)} %all-gather.5.cloned.1.call-done, bf16[5120,1024]{1,0:T(8,128)(2,1)} %param.15), kind=kOutput, calls=%fused_computation.48 | convolution fusion | flops 1342308352 | bytes 12058624 | tf_op jit(solution)/shard_map/dot_general | solution.py:68
  40.6 6.2 %convolution_convert_fusion.1 = bf16[128,1024]{1,0:T(8,128)(2,1)} fusion(bf16[128,5120]{1,0:T(8,128)(2,1)S(1)} %copy-done, bf16[5120,1024]{1,0:T(8,128)(2,1)} %param.17), kind=kOutput, calls=%fused_computation.46 | convolution fusion | flops 1342308352 | bytes 12058624 | tf_op jit(solution)/shard_map/dot_general | solution.py:68
  46.9 42.9 %all-gather.7.cloned.1.call-done = bf16[1024,1024]{1,0:T(8,128)(2,1)} async-done(((bf16[128,1024]{1,0:T(8,128)(2,1)}), bf16[1024,1024]{1,0:T(8,128)(2,1)}) %all-gather.7.cloned.1.call-update) | async-done | bytes 2097168 | tf_op jit(solution)/shard_map/all_gather | solution.py:87
  92.0 38.5 %while.15 = (s32[]{:T(128)}, f32[8,8,128]{2,1,0:T(8,128)S(1)}, f32[8,8,128]{2,1,0:T(8,128)S(1)}, f32[8,8,128,128]{3,2,1,0:T(8,128)}, bf16[8,128,8,128]{3,2,1,0:T...) while((s32[]{:T(128)}, f32[8,8,128]{2,1,0:T(8,128)S(1)}, ...), condition=%wide.region_6.7_spmd.clone, body=%wide.region_3.6_spmd.clone.sunk | while | flops 136713728 | bytes 5555829 | solution.py:94
  99.0 2.2 fusion.91
  103.8 2.2 fusion.91
  108.6 2.2 fusion.91
  113.4 2.2 fusion.91
  118.3 2.2 fusion.91
  127.8 2.2 fusion.91
  130.5 9.8 %all_to_all.15 = f32[8,8,128]{2,1,0:T(8,128)S(1)} all-to-all(f32[8,8,128]{2,1,0:T(8,128)S(1)} %get-tuple-element.50), channel_id=1, replica_groups=mesh['span'=8,'tensor'=4] {'span'}, dimensions={0} | all-to-all | bytes 65536 | tf_op jit(solution)/shard_map/all_to_all | solution.py:95
  140.3 9.0 %all_to_all.16 = f32[8,8,128]{2,1,0:T(8,128)S(1)} all-to-all(f32[8,8,128]{2,1,0:T(8,128)S(1)} %get-tuple-element.51), channel_id=1, replica_groups=mesh['span'=8,'tensor'=4] {'span'}, dimensions={0} | all-to-all | bytes 65536 | tf_op jit(solution)/shard_map/all_to_all | solution.py:95
  149.4 4.5 %all-to-all-start = ((f32[8,8,128,128]{3,2,1,0:T(8,128)}), f32[8,8,128,128]{3,2,1,0:T(8,128)}, u32[]{:S(2)}, u32[]{:S(2)}) async-start(f32[8,8,128,128]{3,2,1,0:T(8,128)} %get-tuple-element.49), calls=%async_computation | async-start | bytes 8388608 | tf_op jit(solution)/shard_map/all_to_all | solution.py:95
  154.0 6.2 %convolution_convert_fusion.2 = bf16[128,1024]{1,0:T(8,128)(2,1)} fusion(bf16[128,5120]{1,0:T(8,128)(2,1)S(1)} %copy-done, bf16[5120,1024]{1,0:T(8,128)(2,1)} %param.16), kind=kOutput, calls=%fused_computation.47 | convolution fusion | flops 1342308352 | bytes 12058624 | tf_op jit(solution)/shard_map/dot_general | solution.py:68
  161.7 2.9 copy.32
  164.6 92.7 %all-gather.9.cloned.1.call-done = bf16[1024,1024]{1,0:T(8,128)(2,1)} async-done(((bf16[128,1024]{1,0:T(8,128)(2,1)}), bf16[1024,1024]{1,0:T(8,128)(2,1)}) %all-gather.9.cloned.1.call-update) | async-done | bytes 2097168 | tf_op jit(solution)/shard_map/all_gather | solution.py:105
  257.3 4.5 %fusion.19 = (f32[8,128]{1,0:T(8,128)S(1)}, f32[8,128,1024]{2,1,0:T(8,128)}) fusion(pred[1024]{0:T(1024)(128)(4,1)S(1)} %broadcast_compare_fusion, bf16[1024,1024]{1,0:T(8,128)(2,1)} %all-gather.9.cloned.1.call-done, bf16[128,1024]{1,0:T(8,128)(2,1)S(1)} %copy-done.1), kind=kOutput, calls=%fused_computation.32 | convolution fusion | flops 271580160 | bytes 6558720 | tf_op jit(solution)/shard_map/qhd,khd->hqk/dot_general | solution.py:18
  261.8 3.3 %fusion.20 = f32[8,128]{1,0:T(8,128)S(1)} fusion(f32[8,128,1024]{2,1,0:T(8,128)} %get-tuple-element.133, f32[8,128]{1,0:T(8,128)S(1)} %max.18, pred[1024]{0:T(1024)(128)(4,1)S(1)} %broadcast_compare_fusion), kind=kLoop, calls=%fused_computation.33 | loop fusion | flops 5241856 | bytes 4203520 | tf_op jit(solution)/shard_map/reduce_sum | solution.py:25
  265.1 4.8 %all-to-all-done = f32[8,8,128,128]{3,2,1,0:T(8,128)} async-done(((f32[8,8,128,128]{3,2,1,0:T(8,128)}), f32[8,8,128,128]{3,2,1,0:T(8,128)}, u32[]{:S(2)}, u32[]{:S(2)}) %all-to-all-start) | async-done | bytes 4194336 | tf_op jit(solution)/shard_map/all_to_all | solution.py:95
  269.9 2.9 multiply_reduce_fusion
  273.0 3.6 %fusion.41 = bf16[128,8,128]{0,2,1:T(8,128)(2,1)S(1)} fusion(bf16[1024,8,128]{0,2,1:T(8,128)(2,1)S(1)} %bitcast.117, f32[8,128,1024]{2,1,0:T(8,128)} %get-tuple-element.133, f32[8,128]{1,0:T(8,128)S(1)} %max.18, pred[1024]{0:T(1024)(128)(4,1)S(1)} %broadcast_compare_fusion, f32[8,128,128]{1,2,0:T(8,128)S(1)} %copy.28, f32[128,8]{0,1:T(8,128)S(1)} %get-tuple-element.119, ...), kind=kOutput, calls=%fused_computation.50 | convolution fusion | flops 274202624 | bytes 7091200 | tf_op jit(solution)/shard_map/hqk,khd->hqd/dot_general | solution.py:26
  276.6 6.6 %convolution_convert_fusion = bf16[128,5120]{1,0:T(8,128)(2,1)} fusion(bf16[128,1024]{0,1:T(8,128)(2,1)S(1)} %bitcast.119, bf16[1024,5120]{1,0:T(8,128)(2,1)} %param.18), kind=kOutput, calls=%fused_computation.28 | convolution fusion | flops 1342832640 | bytes 12058624 | tf_op jit(solution)/shard_map/dot_general | solution.py:121
  283.2 25.5 %reduce-scatter.2.cloned.1.call-done = bf16[32,5120]{1,0:T(8,128)(2,1)} async-done(((bf16[128,5120]{1,0:T(8,128)(2,1)}), bf16[32,5120]{1,0:T(8,128)(2,1)}) %reduce-scatter.2.cloned.1.call-update) | async-done | bytes 327696 | tf_op jit(solution)/shard_map/reduce_scatter | solution.py:120
  (89 shorter events, 36.0 us)
Async XLA Ops:
  6.5 27.3 %all-gather.5.cloned.1.call-start = ((), (), s32[]{:S(2)}) async-start(), calls=%async_computation.4 | async-start | bytes 1638400 | tf_op jit(solution)/shard_map/all_gather | solution.py:66
  12.7 77.0 %all-gather.7.cloned.1.call-start = ((), (), s32[]{:S(2)}) async-start(), calls=%async_computation.5 | async-start | bytes 2359296 | tf_op jit(solution)/shard_map/all_gather | solution.py:87
  33.8 6.8 %copy-start = (bf16[128,5120]{1,0:T(8,128)(2,1)S(1)}, bf16[128,5120]{1,0:T(8,128)(2,1)}, u32[]{:S(2)}) copy-start(bf16[128,5120]{1,0:T(8,128)(2,1)} %all-gather.5.cloned.1.call-done) | copy-start | bytes 3932164
  40.5 121.2 %all-gather.11.cloned.1.call-start = ((), (), s32[]{:S(2)}) async-start(), calls=%async_computation.7 | async-start | bytes 2359296 | tf_op jit(solution)/shard_map/all_gather | solution.py:106
  149.4 120.5 %all-to-all-start = ((f32[8,8,128,128]{3,2,1,0:T(8,128)}), f32[8,8,128,128]{3,2,1,0:T(8,128)}, u32[]{:S(2)}, u32[]{:S(2)}) async-start(f32[8,8,128,128]{3,2,1,0:T(8,128)} %get-tuple-element.49), calls=%async_computation | async-start | bytes 8388608 | tf_op jit(solution)/shard_map/all_to_all | solution.py:95
  153.9 6.6 %copy-start.2 = (s32[8]{0:T(128)S(1)}, s32[8]{0:T(128)}, u32[]{:S(2)}) copy-start(s32[8]{0:T(128)} %param.22) | copy-start | bytes 100
  153.9 103.4 %all-gather.9.cloned.1.call-start = ((), (), s32[]{:S(2)}) async-start(), calls=%async_computation.6 | async-start | bytes 2359296 | tf_op jit(solution)/shard_map/all_gather | solution.py:105
  160.2 97.1 %copy-start.1 = (bf16[128,1024]{1,0:T(8,128)(2,1)S(1)}, bf16[128,1024]{1,0:T(8,128)(2,1)}, u32[]{:S(2)}) copy-start(bf16[128,1024]{1,0:T(8,128)(2,1)} %convolution_convert_fusion.3) | copy-start | bytes 786436
  160.2 148.5 %reduce-scatter.2.cloned.1.call-start = ((), (), s32[]{:S(2)}) async-start(), calls=%async_computation.8 | async-start | bytes 1638400 | tf_op jit(solution)/shard_map/reduce_scatter | solution.py:120
Sparse Core Ops, SparseCore 0:
  12.9 20.8 all-gather.4
  40.7 49.0 all-gather.6
  91.9 48.4 all-gather.10
  160.3 96.8 all-gather.8
  283.3 25.3 reduce-scatter.1
where the time goes:
time: 319 us; the launch traced here: 317 us
  waiting for transfers between devices  187 us (59%)
  matrix products  63.2 us (20%)
  other arithmetic  23.1 us (7%)
  blocking collectives  18.9 us (6%)
  between operations  14 us (4%)
  local copies, waits for them, and re-layouts  5.46 us (2%)
  starting transfers between devices  4.89 us (2%)
    all_gather x1, waiting for transfers between devices, body(): key_rows = lax.all_gather(own_key, 'span', axis=0, tiled=True)  92.7 us
    all_gather x1, waiting for transfers between devices, body(): all_queries = lax.all_gather(own_query, 'span', axis=0, tiled=True)  42.9 us
    reduce_scatter x1, waiting for transfers between devices, body(): lax.psum_scatter(jnp.dot(attended, w_out, preferred_element_type=jnp.floa...  25.5 us
    dot_general x9, matrix products, block_update(): jnp.einsum('hqk,khd->hqd', weights.astype(jnp.bfloat16), value_heads, pre...  21.4 us
    all_gather x1, waiting for transfers between devices, body(): shard_piece = lax.all_gather(modulated, 'tensor', axis=0, tiled=True)  21 us
    dot_general x3, matrix products, body(): jnp.dot(shard_piece, weight, preferred_element_type=jnp.float32)  19.1 us
    all_to_all x2, blocking collectives, body(): lax.all_to_all(partials, 'span', split_axis=0, concat_axis=0, tiled=True)  18.9 us
    dot_general x9, matrix products, block_update(): jnp.einsum('qhd,khd->hqk', q_heads, key_heads, preferred_element_type=jnp...  16.1 us
  transfers between devices with their start and end apart: 6, of which 5 were waited for; matrix products, arithmetic and copies ran while one was open for 20% of the time, Pallas kernels for 0%

commit v1 on v0

--- a/solution.py
+++ b/solution.py
@@ -1,6 +1,10 @@
+import functools
+
 import jax
 import jax.numpy as jnp
 from jax import lax
+from jax.experimental import pallas as pl
+from jax.experimental.pallas import tpu as pltpu
 from jax.sharding import PartitionSpec as P
 
 HD = 128
@@ -37,7 +41,7 @@
     return running
 
 
-def body(
+def general_body(
     latents,
     modulation,
     w_query,
@@ -126,6 +130,264 @@
     return (gate_row[None, :] * projection).astype(jnp.bfloat16)
 
 
+NEG = -1e30
+LOG2E = 1.4426950408889634
+
+
+def whole(shape):
+    return pl.BlockSpec(shape, lambda *_: (0,) * len(shape))
+
+
+def project_kernel(level_ref, *refs, blocks, weights, chunk):
+    x_refs = refs[:blocks]
+    mod_ref = refs[blocks]
+    w_refs = refs[blocks + 1 : blocks + 1 + weights]
+    out_ref = refs[blocks + 1 + weights]
+    xn_ref, acc_ref, wbuf, sems = refs[blocks + 2 + weights :]
+    slots = wbuf.shape[0]
+    depth = w_refs[0].shape[0]
+    steps = depth // chunk
+
+    def fetch(weight, step, slot):
+        return pltpu.make_async_copy(
+            w_refs[weight].at[pl.ds(step * chunk, chunk)], wbuf.at[slot], sems.at[slot]
+        )
+
+    total = weights * steps
+    for index in range(slots):
+        fetch(index // steps, index % steps, index).start()
+    rows = x_refs[0].shape[0]
+    shift = mod_ref[0, 0:1, :]
+    scale = 1.0 + mod_ref[0, 1:2, :]
+    for index, x_ref in enumerate(x_refs):
+        data = x_ref[...].astype(jnp.float32)
+        mean = jnp.sum(data, axis=-1, keepdims=True) * (1.0 / depth)
+        centred = data - mean
+        var = jnp.sum(centred * centred, axis=-1, keepdims=True) * (1.0 / depth)
+        normed = centred * lax.rsqrt(var + EPSILON)
+        mixed = (normed * scale + shift).astype(jnp.bfloat16)
+        for step in range(steps):
+            xn_ref[step, pl.ds(index * rows, rows), :] = mixed[:, step * chunk : (step + 1) * chunk]
+    heads = out_ref.shape[0]
+    for weight in range(weights):
+        acc_ref[...] = jnp.zeros_like(acc_ref)
+
+        def one(step, carry, weight=weight):
+            index = weight * steps + step
+            slot = lax.rem(index, slots)
+            fetch(weight, step, slot).wait()
+            acc_ref[...] += jnp.dot(
+                xn_ref[step], wbuf[slot], preferred_element_type=jnp.float32
+            )
+            ahead = index + slots
+            for later in range(weight, weights):
+
+                @pl.when((ahead >= later * steps) & (ahead < (later + 1) * steps))
+                def _(later=later):
+                    fetch(later, ahead - later * steps, slot).start()
+
+            return carry
+
+        lax.fori_loop(0, steps, one, 0)
+        for head in range(heads):
+            out_ref[head, weight] = acc_ref[:, head * HD : (head + 1) * HD].astype(jnp.bfloat16)
+
+
+def project(level, blocks, modulation, weight_list, chunk=640, slots=4):
+    rows, depth = blocks[0].shape
+    span_rows = rows * len(blocks)
+    width = weight_list[0].shape[1]
+    heads = width // HD
+    count = len(weight_list)
+    steps = depth // chunk
+    return pl.pallas_call(
+        functools.partial(
+            project_kernel, blocks=len(blocks), weights=count, chunk=chunk
+        ),
+        grid_spec=pltpu.PrefetchScalarGridSpec(
+            num_scalar_prefetch=1,
+            grid=(1,),
+            in_specs=[whole((rows, depth))] * len(blocks)
+            + [pl.BlockSpec((1,) + modulation.shape[1:], lambda i, lv: (lv[0], 0, 0))]
+            + [pl.BlockSpec(memory_space=pl.ANY)] * count,
+            out_specs=whole((heads, count, span_rows, HD)),
+            scratch_shapes=[
+                pltpu.VMEM((steps, span_rows, chunk), jnp.bfloat16),
+                pltpu.VMEM((span_rows, width), jnp.float32),
+                pltpu.VMEM((slots, chunk, width), jnp.bfloat16),
+                pltpu.SemaphoreType.DMA((slots,)),
+            ],
+        ),
+        out_shape=jax.ShapeDtypeStruct((heads, count, span_rows, HD), jnp.bfloat16),
+        compiler_params=pltpu.CompilerParams(vmem_limit_bytes=24 << 20),
+        cost_estimate=pl.CostEstimate(
+            flops=2 * span_rows * depth * width * count,
+            bytes_accessed=2 * depth * width * count,
+            transcendentals=0,
+        ),
+        name="project",
+    )(level, *blocks, modulation, *weight_list)
+
+
+def attend_kernel(rot_ref, live_ref, qkv_ref, cache_ref, out_ref):
+    groups = qkv_ref.shape[0]
+    span = pl.program_id(0)
+    span_rows = qkv_ref.shape[2]
+    cache_rows = cache_ref.shape[0] * cache_ref.shape[2]
+    new_rows = groups * span_rows
+    q = qkv_ref[span, 0]
+    dims = (((1,), (1,)), ((), ()))
+    keys = cache_ref[:, 0].reshape(cache_rows, HD)
+    s_cache = lax.dot_general(q, keys, dims, preferred_element_type=jnp.float32)
+    place = lax.broadcasted_iota(jnp.int32, (1, cache_rows), 1)
+    s_cache = s_cache + jnp.where(place < live_ref[0], 0.0, NEG)
+    s_new = lax.dot_general(
+        q, qkv_ref[:, 1].reshape(new_rows, HD), dims, preferred_element_type=jnp.float32
+    )
+    own = rot_ref[span]
+    bias = jnp.concatenate(
+        [
+            jnp.full((1, span_rows), jnp.where(rot_ref[other] <= own, 0.0, NEG), jnp.float32)
+            for other in range(groups)
+        ],
+        axis=1,
+    )
+    s_new = s_new + bias
+    top = jnp.maximum(
+        jnp.max(s_cache, axis=1, keepdims=True), jnp.max(s_new, axis=1, keepdims=True)
+    )
+    factor = HD**-0.5 * LOG2E
+    p_cache = jnp.exp2((s_cache - top) * factor)
+    p_new = jnp.exp2((s_new - top) * factor)
+    total = jnp.sum(p_cache, axis=1, keepdims=True) + jnp.sum(p_new, axis=1, keepdims=True)
+    acc = jnp.dot(
+        p_cache.astype(jnp.bfloat16),
+        cache_ref[:, 1].reshape(cache_rows, HD),
+        preferred_element_type=jnp.float32,
+    ) + jnp.dot(
+        p_new.astype(jnp.bfloat16),
+        qkv_ref[:, 2].reshape(new_rows, HD),
+        preferred_element_type=jnp.float32,
+    )
+    out_ref[0] = (acc / total).astype(jnp.bfloat16)
+
+
+def attend_all(rotation, live, qkv, cache):
+    groups, _, span_rows, _ = qkv.shape
+    cache_rows = cache.shape[0] * cache.shape[2]
+    keys = cache_rows + groups * span_rows
+    return pl.pallas_call(
+        attend_kernel,
+        grid_spec=pltpu.PrefetchScalarGridSpec(
+            num_scalar_prefetch=2,
+            grid=(groups,),
+            in_specs=[whole(qkv.shape), whole(cache.shape)],
+            out_specs=pl.BlockSpec((1, span_rows, HD), lambda g, *_: (g, 0, 0)),
+        ),
+        out_shape=jax.ShapeDtypeStruct((groups, span_rows, HD), jnp.bfloat16),
+        compiler_params=pltpu.CompilerParams(vmem_limit_bytes=32 << 20),
+        cost_estimate=pl.CostEstimate(
+            flops=4 * groups * span_rows * keys * HD,
+            bytes_accessed=2 * (qkv.size + cache.size),
+            transcendentals=groups * span_rows * keys,
+        ),
+        name="attend",
+    )(rotation, live, qkv, cache)
+
+
+def out_kernel(o_ref, w_ref, keep_ref, send_ref):
+    heads, span_rows, _ = o_ref.shape
+    lhs = jnp.concatenate([o_ref[head] for head in range(heads)], axis=1)
+    result = jnp.dot(lhs, w_ref[...], preferred_element_type=jnp.float32)
+    half, rows, _ = keep_ref.shape
+    for index in range(half):
+        keep_ref[index] = result[2 * index * rows : (2 * index + 1) * rows]
+        send_ref[index] = result[(2 * index + 1) * rows : (2 * index + 2) * rows].astype(
+            jnp.bfloat16
+        )
+
+
+def out_project(attended, w_out, blocks, chunk=640):
+    heads, span_rows, _ = attended.shape
+    width = w_out.shape[1]
+    rows = span_rows // blocks
+    half = blocks // 2
+    spec = pl.BlockSpec((half, rows, chunk), lambda j: (0, 0, j))
+    return pl.pallas_call(
+        out_kernel,
+        grid=(width // chunk,),
+        in_specs=[
+            whole(attended.shape),
+            pl.BlockSpec((heads * HD, chunk), lambda j: (0, j)),
+        ],
+        out_specs=[spec, spec],
+        out_shape=[
+            jax.ShapeDtypeStruct((half, rows, width), jnp.float32),
+            jax.ShapeDtypeStruct((half, rows, width), jnp.bfloat16),
+        ],
+        compiler_params=pltpu.CompilerParams(vmem_limit_bytes=24 << 20),
+        cost_estimate=pl.CostEstimate(
+            flops=2 * span_rows * heads * HD * width,
+            bytes_accessed=2 * heads * HD * width,
+            transcendentals=0,
+        ),
+        name="out_project",
+    )(attended, w_out)
+
+
+def swap(value, bit, size):
+    return lax.ppermute(value, "tensor", [(place, place ^ bit) for place in range(size)])
+
+
+def fast_body(
+    latents,
+    modulation,
+    w_query,
+    w_key,
+    w_value,
+    w_out,
+    cache_k,
+    cache_v,
+    level_index,
+    rotation,
+    cached_tokens,
+):
+    groups = lax.axis_size("span")
+    tensor = lax.axis_size("tensor")
+    cache_rows = cache_k.shape[0]
+    packed = jnp.stack(
+        [part.reshape(cache_rows, groups, HD).transpose(1, 0, 2) for part in (cache_k, cache_v)],
+        axis=1,
+    )
+    cache = lax.all_to_all(packed, "span", split_axis=0, concat_axis=0, tiled=True)
+    blocks = [latents]
+    bit = tensor // 2
+    order = [0]
+    while bit:
+        blocks = blocks + [swap(block, bit, tensor) for block in blocks]
+        order = order + [place ^ bit for place in order]
+        bit //= 2
+    blocks = [blocks[order.index(place)] for place in range(tensor)]
+    qkv = project(level_index, blocks, modulation, [w_query, w_key, w_value])
+    qkv = lax.all_to_all(qkv, "span", split_axis=0, concat_axis=0, tiled=True)
+    attended = attend_all(rotation, cached_tokens, qkv, cache)
+    attended = lax.all_to_all(attended, "span", split_axis=0, concat_axis=0, tiled=True)
+    keep, send = out_project(attended, w_out, tensor)
+    parts = [None] * (tensor // 2)
+    for index in reversed(range(tensor // 2)):
+        parts[index] = keep[index] + swap(send[index], 1, tensor).astype(jnp.float32)
+    bit = 2
+    while bit < tensor:
+        stay, go = parts[0::2], parts[1::2]
+        parts = [
+            mine + swap(other.astype(jnp.bfloat16), bit, tensor).astype(jnp.float32)
+            for mine, other in zip(stay, go)
+        ]
+        bit *= 2
+    gate = lax.dynamic_slice_in_dim(modulation[:, 2, :], level_index[0], 1, axis=0)
+    return (gate * parts[0]).astype(jnp.bfloat16)
+
+
 def solution(mesh):
     placed = (
         P(("span", "tensor"), None),
@@ -140,6 +402,15 @@
         P(),
         P(),
     )
+
+    def body(*args):
+        groups = mesh.shape["span"]
+        tensor = mesh.shape["tensor"]
+        heads = args[2].shape[1] // HD
+        if heads == groups and tensor >= 2 and tensor & (tensor - 1) == 0:
+            return fast_body(*args)
+        return general_body(*args)
+
     return jax.shard_map(
         body, mesh=mesh, in_specs=placed, out_specs=P(("span", "tensor"), None), check_vma=False
     )

time: 319 us -> 114 us (0.36)
  waiting for transfers between devices: 187 us -> 37.3 us
  matrix products: 63.2 us -> 0 us
  Pallas kernels: 0 us -> 25.9 us
  other arithmetic: 23.1 us -> 1.99 us
  between operations: 14 us -> 1.45 us
  starting transfers between devices: 4.89 us -> 16.8 us
  local copies, waits for them, and re-layouts: 5.46 us -> 17.1 us
  blocking collectives: 18.9 us -> 12.6 us
    all_gather x4 -> x0, waiting for transfers between devices: 157 us -> none  [the longest x1 92.7 us: body(): key_rows = lax.all_gather(own_key, 'span', axis=0, tiled=True)]
    dot_general x22 -> x0, matrix products: 63.2 us -> none  [the longest x9 21.4 us: block_update(): jnp.einsum('hqk,khd->hqd', weights.astype(jnp.bfloat16), value_heads, pre...]
    pallas_call x0 -> x3, Pallas kernels: none -> 25.9 us  [the longest x1 13.5 us: project(): pl.pallas_call(functools.partial(project_kernel, blocks=len(blocks), weig...]
    reduce_scatter x1 -> x0, waiting for transfers between devices: 25.5 us -> none  [body(): lax.psum_scatter(jnp.dot(attended, w_out, preferred_element_type=jnp.floa...]
    ppermute x0 -> x6, waiting for transfers between devices: none -> 17.2 us  [swap(): lax.ppermute(value, 'tensor', [(place, place ^ bit) for place in range(si...]
    all_to_all x1 -> x2, waiting for transfers between devices: 4.79 us -> 20.2 us  [the longest x1 20.2 us: fast_body(): qkv = lax.all_to_all(qkv, 'span', split_axis=0, concat_axis=0, tiled=True)]
    unnamed x7 -> x13, local copies, waits for them, and re-layouts: 2.22 us -> 16.5 us
    reduce_sum x16 -> x0, other arithmetic: 13.5 us -> none  [the longest x9 6.34 us: block_update(): run_sum = run_sum * rescale + jnp.sum(weights, axis=-1)]
  transfers between devices with their start and end apart: 6 -> 8, of which waited for: 5 -> 4; matrix products, arithmetic and copies ran while one was open for 20% -> 1% of each run, Pallas kernels for 0% -> 12%
where the time goes in v1:
time: 114 us; the launch traced here: 113 us
  waiting for transfers between devices  37.3 us (33%)
  Pallas kernels  25.9 us (23%)
  local copies, waits for them, and re-layouts  17.1 us (15%)
  starting transfers between devices  16.8 us (15%)
  blocking collectives  12.6 us (11%)
  other arithmetic  1.99 us (2%)
  between operations  1.45 us (1%)
    all_to_all x1, waiting for transfers between devices, fast_body(): qkv = lax.all_to_all(qkv, 'span', split_axis=0, concat_axis=0, tiled=True)  20.2 us
    ppermute x6, waiting for transfers between devices, swap(): lax.ppermute(value, 'tensor', [(place, place ^ bit) for place in range(si...  17.2 us
    unnamed x13, local copies, waits for them, and re-layouts  16.5 us
    pallas_call x1, Pallas kernels, project(): pl.pallas_call(functools.partial(project_kernel, blocks=len(blocks), weig...  13.5 us
    all_to_all x1, blocking collectives, fast_body(): lax.all_to_all(attended, 'span', split_axis=0, concat_axis=0, tiled=True)  12.6 us
    pallas_call x1, Pallas kernels, attend_all(): pl.pallas_call(attend_kernel, grid_spec=pltpu.PrefetchScalarGridSpec(num_...  8.01 us
    all_to_all x1, starting transfers between devices, fast_body(): lax.all_to_all(packed, 'span', split_axis=0, concat_axis=0, tiled=True)  7.28 us
    all_to_all x1, starting transfers between devices, fast_body(): qkv = lax.all_to_all(qkv, 'span', split_axis=0, concat_axis=0, tiled=True)  5.87 us
  transfers between devices with their start and end apart: 8, of which 4 were waited for; matrix products, arithmetic and copies ran while one was open for 1% of the time, Pallas kernels for 12%

profile of v1, /device:TPU:0, one launch (start us, length us, event | category | flops | bytes accessed | tf_op | source)
XLA Modules:
  0.0 113.2 jit_solution(8635925866644601578)
XLA Ops:
  0.0 1.2 %copy.14 = bf16[256,1024]{0,1:T(8,128)(2,1)S(1)} copy(bf16[256,1024]{1,0:T(8,128)(2,1)} %param.17) | data formatting | bytes 1048576 | tf_op args[6]
  1.2 0.3 copy.15
  1.5 1.2 %copy.16 = bf16[256,1024]{0,1:T(8,128)(2,1)S(1)} copy(bf16[256,1024]{1,0:T(8,128)(2,1)} %param.18) | data formatting | bytes 1048576 | tf_op args[7]
  2.8 0.3 copy.17
  3.1 1.1 pad_maximum_fusion
  4.1 7.3 %all-to-all-start.1 = ((bf16[8,2,256,128]{3,2,1,0:T(8,128)(2,1)}), bf16[8,2,256,128]{3,2,1,0:T(8,128)(2,1)S(1)}, u32[]{:S(2)}, u32[]{:S(2)}) async-start(bf16[8,2,256,128]{3,2,1,0:T(8,128)(2,1)} %pad_maximum_fusion), calls=%async_computation.1 | async-start | bytes 2097152 | tf_op jit(solution)/shard_map/all_to_all | solution.py:362
  11.4 1.5 %collective-permute-start.1 = (bf16[32,5120]{1,0:T(8,128)(2,1)}, bf16[32,5120]{1,0:T(8,128)(2,1)S(1)}, u32[]{:S(2)}, u32[]{:S(2)}) collective-permute-start(bf16[32,5120]{1,0:T(8,128)(2,1)} %refs_0_.1), channel_id=1, source_target_pairs={{0,2},{1,3},{2,0},{3,1},{4,6},{5,7},{6,4},{7,5},{8,10},{9,11},{10,... | collective-permute-start | bytes 983048 | tf_op jit(solution)/shard_map/ppermute | solution.py:339
  12.9 7.9 %collective-permute-done.1.refs_2_ = bf16[32,5120]{1,0:T(8,128)(2,1)S(1)} collective-permute-done((bf16[32,5120]{1,0:T(8,128)(2,1)}, bf16[32,5120]{1,0:T(8,128)(2,1)S(1)}, u32[]{:S(2)}, u32[]{:S(2)}) %collective-permute-start.1) | collective-permute-done | bytes 327712 | tf_op jit(solution)/shard_map/ppermute | solution.py:339
  21.5 1.1 copy.13.refs_4_
  22.6 4.0 %copy-done = bf16[5120,1024]{1,0:T(8,128)(2,1)S(1)} copy-done((bf16[5120,1024]{1,0:T(8,128)(2,1)S(1)}, bf16[5120,1024]{1,0:T(8,128)(2,1)}, u32[]{:S(2)}) %copy-start) | copy-done | bytes 10485784
  26.6 4.0 %copy-done.1 = bf16[5120,1024]{1,0:T(8,128)(2,1)S(1)} copy-done((bf16[5120,1024]{1,0:T(8,128)(2,1)S(1)}, bf16[5120,1024]{1,0:T(8,128)(2,1)}, u32[]{:S(2)}) %copy-start.1) | copy-done | bytes 10485784
  30.6 1.0 copy-done.3
  31.5 13.5 %project.1 = bf16[8,3,128,128]{3,2,1,0:T(8,128)(2,1)} custom-call(s32[1]{0:T(128)} %copy.18.level_ref, bf16[32,5120]{1,0:T(8,128)(2,1)S(1)} %copy-done.3, bf16[32,5120]{1,0:T(8,128)(2,1)S(1)} %collective-permute-done.refs_1_, bf16[32,5120]{1,0:T(8,128)(2,1)S(1)} %collective-permute-done.1.refs_2_, bf16[32,5120]{1,0:T(8,128)(2,1)S(1)} %collective-permute-done.2.refs_3_, ...), custom_call_target="tpu_custom_call" | custom-call | flops 4026531840 | bytes 31457280 | tf_op jit(solution)/shard_map/project/pallas_call | solution.py:203
  45.1 5.9 %all-to-all-start = ((bf16[8,3,128,128]{3,2,1,0:T(8,128)(2,1)}), bf16[8,3,128,128]{3,2,1,0:T(8,128)(2,1)S(1)}, u32[]{:S(2)}, u32[]{:S(2)}) async-start(bf16[8,3,128,128]{3,2,1,0:T(8,128)(2,1)} %project.1), calls=%async_computation | async-start | bytes 1572864 | tf_op jit(solution)/shard_map/all_to_all | solution.py:372
  51.6 20.2 %all-to-all-done.qkv_ref = bf16[8,3,128,128]{3,2,1,0:T(8,128)(2,1)S(1)} async-done(((bf16[8,3,128,128]{3,2,1,0:T(8,128)(2,1)}), bf16[8,3,128,128]{3,2,1,0:T(8,128)(2,1)S(1)}, u32[]{:S(2)}, u32[]{:S(2)}) %all-to-all-start) | async-done | bytes 786464 | tf_op jit(solution)/shard_map/all_to_all | solution.py:372
  71.8 8.0 %attend.1 = bf16[8,128,128]{2,1,0:T(8,128)(2,1)S(1)} custom-call(s32[8]{0:T(128)S(1)} %copy-done.4, s32[1]{0:T(128)S(6)} %copy.19.live_ref, bf16[8,3,128,128]{3,2,1,0:T(8,128)(2,1)S(1)} %all-to-all-done.qkv_ref, bf16[8,2,256,128]{3,2,1,0:T(8,128)(2,1)S(1)} %all-to-all-done.1.cache_ref), custom_call_target="tpu_custom_call" | custom-call | flops 1610612736 | bytes 1835008 | tf_op jit(solution)/shard_map/attend/pallas_call | solution.py:279
  79.8 12.6 %all_to_all.15.o_ref = bf16[8,128,128]{2,1,0:T(8,128)(2,1)S(1)} all-to-all(bf16[8,128,128]{2,1,0:T(8,128)(2,1)S(1)} %attend.1), channel_id=1, replica_groups=mesh['span'=8,'tensor'=4] {'span'}, dimensions={0} | all-to-all | bytes 524288 | tf_op jit(solution)/shard_map/all_to_all | solution.py:374
  92.3 4.0 %copy-done.2 = bf16[1024,5120]{1,0:T(8,128)(2,1)S(1)} copy-done((bf16[1024,5120]{1,0:T(8,128)(2,1)S(1)}, bf16[1024,5120]{1,0:T(8,128)(2,1)}, u32[]{:S(2)}) %copy-start.2) | copy-done | bytes 10485784
  96.3 4.4 %out_project.1 = (f32[2,32,5120]{2,1,0:T(8,128)S(1)}, bf16[2,32,5120]{2,1,0:T(8,128)(2,1)S(1)}) custom-call(bf16[8,128,128]{2,1,0:T(8,128)(2,1)S(1)} %all_to_all.15.o_ref, bf16[1024,5120]{1,0:T(8,128)(2,1)S(1)} %copy-done.2), custom_call_target="tpu_custom_call" | custom-call | flops 1342177280 | bytes 10485760 | tf_op jit(solution)/shard_map/out_project/pallas_call | solution.py:316
  100.8 0.5 collective-permute-start.3
  101.3 1.1 collective-permute-done.4
  102.5 1.6 %collective-permute-start.5 = (bf16[32,5120]{1,0:T(8,128)(2,1)S(1)}, bf16[32,5120]{1,0:T(8,128)(2,1)S(1)}, u32[]{:S(2)}, u32[]{:S(2)}) collective-permute-start(bf16[32,5120]{1,0:T(8,128)(2,1)S(1)} %fusion), channel_id=1, source_target_pairs={{0,2},{1,3},{2,0},{3,1},{4,6},{5,7},{6,4},{7,5},{8,10},{9,11},{10,... | collective-permute-start | bytes 983048 | tf_op jit(solution)/shard_map/ppermute | solution.py:339
  104.1 8.2 %collective-permute-done.5 = bf16[32,5120]{1,0:T(8,128)(2,1)S(1)} collective-permute-done((bf16[32,5120]{1,0:T(8,128)(2,1)S(1)}, bf16[32,5120]{1,0:T(8,128)(2,1)S(1)}, u32[]{:S(2)}, u32[]{:S(2)}) %collective-permute-start.5) | collective-permute-done | bytes 327712 | tf_op jit(solution)/shard_map/ppermute | solution.py:339
  112.3 0.8 fusion.3
  (18 shorter events, 0.2 us)
Async XLA Ops:
  4.1 40.9 %all-to-all-start.1 = ((bf16[8,2,256,128]{3,2,1,0:T(8,128)(2,1)}), bf16[8,2,256,128]{3,2,1,0:T(8,128)(2,1)S(1)}, u32[]{:S(2)}, u32[]{:S(2)}) async-start(bf16[8,2,256,128]{3,2,1,0:T(8,128)(2,1)} %pad_maximum_fusion), calls=%async_computation.1 | async-start | bytes 2097152 | tf_op jit(solution)/shard_map/all_to_all | solution.py:362
  11.4 9.4 %collective-permute-start.1 = (bf16[32,5120]{1,0:T(8,128)(2,1)}, bf16[32,5120]{1,0:T(8,128)(2,1)S(1)}, u32[]{:S(2)}, u32[]{:S(2)}) collective-permute-start(bf16[32,5120]{1,0:T(8,128)(2,1)} %refs_0_.1), channel_id=1, source_target_pairs={{0,2},{1,3},{2,0},{3,1},{4,6},{5,7},{6,4},{7,5},{8,10},{9,11},{10,... | collective-permute-start | bytes 983048 | tf_op jit(solution)/shard_map/ppermute | solution.py:339
  12.9 9.7 %collective-permute-start = (bf16[32,5120]{1,0:T(8,128)(2,1)}, bf16[32,5120]{1,0:T(8,128)(2,1)S(1)}, u32[]{:S(2)}, u32[]{:S(2)}) collective-permute-start(bf16[32,5120]{1,0:T(8,128)(2,1)} %refs_0_.1), channel_id=1, source_target_pairs={{0,1},{1,0},{2,3},{3,2},{4,5},{5,4},{6,7},{7,6},{8,9},{9,8},{10,11... | collective-permute-start | bytes 983048 | tf_op jit(solution)/shard_map/ppermute | solution.py:339
  20.8 1.8 %collective-permute-start.2 = (bf16[32,5120]{1,0:T(8,128)(2,1)S(1)}, bf16[32,5120]{1,0:T(8,128)(2,1)S(1)}, u32[]{:S(2)}, u32[]{:S(2)}) collective-permute-start(bf16[32,5120]{1,0:T(8,128)(2,1)S(1)} %collective-permute-done.1.refs_2_), channel_id=1, source_target_pairs={{0,1},{1,0},{2,3},{3,2},{4,5},{5,4},{6,7},{7,6},{8,9},{9,8},{10,11... | collective-permute-start | bytes 983048 | tf_op jit(solution)/shard_map/ppermute | solution.py:339
  21.5 50.3 %copy-start.4 = (s32[8]{0:T(128)S(1)}, s32[8]{0:T(128)}, u32[]{:S(2)}) copy-start(s32[8]{0:T(128)} %rot_ref.1) | copy-start | bytes 100
  22.6 4.0 %copy-start = (bf16[5120,1024]{1,0:T(8,128)(2,1)S(1)}, bf16[5120,1024]{1,0:T(8,128)(2,1)}, u32[]{:S(2)}) copy-start(bf16[5120,1024]{1,0:T(8,128)(2,1)} %refs_5_.1) | copy-start | bytes 31457284
  26.6 4.0 %copy-start.1 = (bf16[5120,1024]{1,0:T(8,128)(2,1)S(1)}, bf16[5120,1024]{1,0:T(8,128)(2,1)}, u32[]{:S(2)}) copy-start(bf16[5120,1024]{1,0:T(8,128)(2,1)} %refs_6_.1) | copy-start | bytes 31457284
  30.6 1.0 copy-start.3
  45.1 59.0 %slice-start = ((f32[4,3,5120]{2,0,1:T(4,128)}), f32[4,1,5120]{2,0,1:T(4,128)S(1)}, s32[]{:S(2)}) async-start(f32[4,3,5120]{2,0,1:T(4,128)} %param.12), calls=%async_computation.3 | async-start | bytes 163840 | tf_op jit(solution)/shard_map/slice | solution.py:387
  45.1 26.7 %all-to-all-start = ((bf16[8,3,128,128]{3,2,1,0:T(8,128)(2,1)}), bf16[8,3,128,128]{3,2,1,0:T(8,128)(2,1)S(1)}, u32[]{:S(2)}, u32[]{:S(2)}) async-start(bf16[8,3,128,128]{3,2,1,0:T(8,128)(2,1)} %project.1), calls=%async_computation | async-start | bytes 1572864 | tf_op jit(solution)/shard_map/all_to_all | solution.py:372
  92.3 4.0 %copy-start.2 = (bf16[1024,5120]{1,0:T(8,128)(2,1)S(1)}, bf16[1024,5120]{1,0:T(8,128)(2,1)}, u32[]{:S(2)}) copy-start(bf16[1024,5120]{1,0:T(8,128)(2,1)} %w_ref.1) | copy-start | bytes 31457284
  100.8 1.7 %collective-permute-start.4 = (bf16[32,5120]{1,0:T(8,128)(2,1)S(1)}, bf16[32,5120]{1,0:T(8,128)(2,1)S(1)}, u32[]{:S(2)}, u32[]{:S(2)}) collective-permute-start(bf16[32,5120]{1,0:T(8,128)(2,1)S(1)} %get-tuple-element.10), channel_id=1, source_target_pairs={{0,1},{1,0},{2,3},{3,2},{4,5},{5,4},{6,7},{7,6},{8,9},{9,8},{10,11... | collective-permute-start | bytes 983048 | tf_op jit(solution)/shard_map/ppermute | solution.py:339
  100.8 3.3 %collective-permute-start.3 = (bf16[32,5120]{1,0:T(8,128)(2,1)S(1)}, bf16[32,5120]{1,0:T(8,128)(2,1)S(1)}, u32[]{:S(2)}, u32[]{:S(2)}) collective-permute-start(bf16[32,5120]{1,0:T(8,128)(2,1)S(1)} %get-tuple-element.9), channel_id=1, source_target_pairs={{0,1},{1,0},{2,3},{3,2},{4,5},{5,4},{6,7},{7,6},{8,9},{9,8},{10,11... | collective-permute-start | bytes 983048 | tf_op jit(solution)/shard_map/ppermute | solution.py:339
  102.5 9.8 %collective-permute-start.5 = (bf16[32,5120]{1,0:T(8,128)(2,1)S(1)}, bf16[32,5120]{1,0:T(8,128)(2,1)S(1)}, u32[]{:S(2)}, u32[]{:S(2)}) collective-permute-start(bf16[32,5120]{1,0:T(8,128)(2,1)S(1)} %fusion), channel_id=1, source_target_pairs={{0,2},{1,3},{2,0},{3,1},{4,6},{5,7},{6,4},{7,5},{8,10},{9,11},{10,... | collective-permute-start | bytes 983048 | tf_op jit(solution)/shard_map/ppermute | solution.py:339
